TPU v7x, 32 devices: a whole 2x2x4 slice. The times are simulated.
32 devices in a mesh: grp: 2 (over x), slc: 16 (over z, y, core).
Axes of the slice: x: 2, y: 2, z: 4, core: 2. Of those that a mesh axis runs over, the one named last changes fastest.
Arguments:
- bitstrings: int32 [1024], P('grp'), parts along dimension 0, may hold values from 0 to 511, as said below
- tree_order: int32 [12], P('grp'), parts along dimension 0, may hold values from 0 to 5, each once
- owners: int32 [12], P('grp'), parts along dimension 0, may hold values from 0 to 15
- slice_assign: int32 [64, 6], P(('grp', 'slc')), parts along dimension 0, may hold values from 0 to 63
- boundary: bfloat16 [1024, 4096], P('grp'), parts along dimension 0, may hold values from -6 to 6
- branch_pool: bfloat16 [32, 64, 4096], P(('grp', 'slc')), parts along dimension 0, may hold values from -0.75 to 0.75
- slice_tensors: bfloat16 [12, 64, 4096], P('grp'), parts along dimension 0, may hold values from -3 to 3
- closing: bfloat16 [8192, 128], P('grp'), parts along dimension 0, may hold values from -0.09375 to 0.09375
Outputs:
- amplitudes: float32 [1024, 128], P(('grp', 'slc')), parts along dimension 0
There are 2 independent parts, one for each index of `grp`. A program takes and returns all parts, laid end to end along the dimension named above; each array names one. Nothing has to cross between parts.
Inputs may be any that keep to these rules, and one draw needn't show every extreme that they name: `bitstrings`: 512 distinct configurations. `tree_order`: a permutation of the sections.
All inputs are finite; a program needn't handle non-finite values.
Results may differ from a plain program's by a relative error of at most 0.0075.
Values may be sent and summed in bfloat16 or wider, within the bound.
A program may use at most 128 MiB of HBM per device.

v0:
```python
import math

import jax
import jax.numpy as jnp
from jax import lax
from jax.sharding import PartitionSpec as P


def spread(block, axis, owner):
    block = jnp.where(lax.axis_index(axis) == owner, block, jnp.zeros_like(block))
    return lax.psum(block, axis)


def local(
    bitstrings, tree_order, owners, slice_assign, boundary, branch_pool, slice_tensors, closing
):
    group_count = lax.axis_size("slc")
    my_index = lax.axis_index("slc")
    slice_count = slice_assign.shape[0]
    bond_dim = branch_pool.shape[1]
    pair_dim = branch_pool.shape[2]
    row_total = bitstrings.shape[0]
    section_count = tree_order.shape[0]
    starts = jnp.take(boundary, bitstrings, axis=0)
    states = jnp.broadcast_to(starts[None], (slice_count, row_total, pair_dim))
    own_branch = branch_pool[0]
    for section_idx in range(section_count):
        branch = spread(own_branch, "slc", owners[section_idx])
        product = jnp.einsum(
            "srab,acb->srcb",
            states.reshape(slice_count, row_total, bond_dim, bond_dim),
            branch.reshape(bond_dim, bond_dim, bond_dim),
            preferred_element_type=jnp.float32,
        )
        table = lax.dynamic_index_in_dim(slice_tensors, tree_order[section_idx], 0, keepdims=False)
        factor = jnp.take(table, slice_assign[:, section_idx], axis=0).astype(jnp.float32)
        states = (product.reshape(slice_count, row_total, pair_dim) * factor[:, None, :]).astype(
            jnp.bfloat16
        )
    inverse = 1.0 / math.sqrt(slice_count * group_count)
    share_rows = row_total // group_count
    partial_amps = jnp.einsum("srw,wo->ro", states, closing, preferred_element_type=jnp.float32)
    totals = lax.psum(partial_amps, "slc")
    summed = lax.dynamic_slice_in_dim(totals, my_index * share_rows, share_rows, 0)
    return summed * inverse


def solution(mesh):
    return jax.shard_map(
        local,
        mesh=mesh,
        in_specs=(
            P("grp"),
            P("grp"),
            P("grp"),
            P(("grp", "slc"), None),
            P("grp", None),
            P(("grp", "slc"), None, None),
            P("grp", None, None),
            P("grp", None),
        ),
        out_specs=P(("grp", "slc"), None),
        check_vma=False,
    )
```

profile of v0, /device:TPU:0, one launch (start us, length us, event | category | flops | bytes accessed | tf_op | source)
XLA Modules:
  0.0 318.7 jit_solution(11319033203107848922)
XLA Ops:
  6.5 1.5 fusion.25
  11.9 2.4 broadcast_select_fusion.6
  14.3 2.1 reshape.99
  16.3 2.9 copy.34
  19.3 2.1 reshape.102
  21.3 2.9 copy.37
  24.2 2.1 reshape.101
  26.3 2.9 copy.36
  29.2 2.1 reshape.100
  31.3 2.9 copy.35
  34.2 1.1 reshape.104
  35.3 2.9 copy.39
  38.2 1.1 reshape.103
  39.4 2.9 copy.38
  42.3 0.2 all-reduce.4.cloned.1.call-start
  42.6 0.7 fusion.24
  50.8 0.3 slice_reduce_fusion.1
  55.0 3.2 dynamic-slice_bitcast_fusion.1
  58.2 1.7 gather_fusion.5
  60.0 0.1 reshape.115
  60.1 0.1 copy.46
  60.2 1.7 gather_fusion.4
  62.0 0.1 reshape.114
  62.1 0.1 copy.45
  62.2 0.6 gather_fusion.3
  62.9 0.1 reshape.113
  63.0 0.1 copy.44
  63.1 0.6 gather_fusion.2
  63.7 0.1 reshape.112
  63.8 0.1 copy.43
  63.9 0.6 gather_fusion.1
  64.6 0.1 reshape.111
  64.7 0.1 copy.42
  64.8 0.6 gather_fusion.6
  65.5 0.1 reshape.116
  65.6 0.1 copy.47
  65.7 11.4 %gather_fusion = bf16[512,4096]{1,0:T(8,128)(2,1)} fusion(bf16[512,4096]{1,0:T(8,128)(2,1)} %param.14, s32[1024]{0:T(1024)S(1)} %pad_clamp_fusion.6), kind=kCustom, calls=%fused_computation.6 | custom fusion | bytes 8390656 | tf_op jit(solution)/shard_map/jit(_take)/gather | solution.py:24
  77.1 6.5 %copy.40 = bf16[512,4096]{0,1:T(8,128)(2,1)} copy(bf16[512,4096]{1,0:T(8,128)(2,1)} %gather_fusion) | data formatting | bytes 8388608 | tf_op jit(solution)/shard_map/jit(_take)/gather | solution.py:24
  83.6 2.7 broadcast_select_fusion
  86.3 4.4 %copy.41 = bf16[512,64,64]{0,1,2:T(8,128)(2,1)} copy(bf16[512,64,64]{0,2,1:T(8,128)(2,1)S(1)} %broadcast_select_fusion) | data formatting | bytes 8388608 | tf_op jit(solution)/shard_map/jit(_take)/select_n | solution.py:24
  90.7 94.3 %all-reduce.6.cloned.1.call-done = (bf16[64,64,64]{0,1,2:T(8,128)(2,1)}, bf16[64,64,64]{0,1,2:T(8,128)(2,1)}, bf16[64,64,64]{0,1,2:T(8,128)(2,1)}, bf16[64,64,64...) async-done(((bf16[64,64,64]{0,1,2:T(8,128)(2,1)}, bf16[64,64,64]{0,1,2:T(8,128)(2,1)}, bf16[64,64,64]{0,1,2:T(8,128)(2,1)}, ...) | async-done | bytes 3145744 | tf_op jit(solution)/shard_map/psum | solution.py:11
  185.0 8.7 %fusion.4 = bf16[2,512,64,64]{1,2,0,3:T(8,128)(2,1)} fusion(f32[2,64,64]{1,0,2:T(2,128)S(1)} %copy.43, f32[2,64,64]{1,0,2:T(2,128)S(1)} %copy.42, bf16[512,64,64]{0,1,2:T(8,128)(2,1)} %copy.41, bf16[64,64,64]{0,1,2:T(8,128)(2,1)} %get-tuple-element.12, bf16[64,64,64]{0,1,2:T(8,128)(2,1)} %get-tuple-element.13), kind=kOutput, calls=%fused_computation.16 | convolution fusion | flops 1090519040 | bytes 13697024 | tf_op jit(solution)/shard_map/srab,acb->srcb/dot_general | solution.py:29
  193.7 9.8 %fusion.2 = bf16[2,512,64,64]{1,2,0,3:T(8,128)(2,1)} fusion(f32[2,64,64]{1,0,2:T(2,128)S(1)} %copy.45, bf16[2,512,64,64]{1,2,0,3:T(8,128)(2,1)} %fusion.4, f32[2,64,64]{1,0,2:T(2,128)S(1)} %copy.44, bf16[64,64,64]{0,1,2:T(8,128)(2,1)S(1)} %copy-done.1, bf16[64,64,64]{0,1,2:T(8,128)(2,1)S(1)} %copy-done.2), kind=kOutput, calls=%fused_computation.12 | convolution fusion | flops 1090519040 | bytes 17891328 | tf_op jit(solution)/shard_map/srab,acb->srcb/dot_general | solution.py:29
  203.5 10.4 %convert_reduce_fusion = bf16[512,64,64]{0,1,2:T(8,128)(2,1)} fusion(f32[2,64,64]{1,0,2:T(2,128)S(1)} %copy.47, bf16[2,512,64,64]{1,2,0,3:T(8,128)(2,1)} %fusion.2, f32[2,64,64]{1,0,2:T(2,128)S(1)} %copy.46, bf16[64,64,64]{0,1,2:T(8,128)(2,1)} %get-tuple-element.16, bf16[64,64,64]{0,1,2:T(8,128)(2,1)} %get-tuple-element.17), kind=kOutput, calls=%fused_computation.19 | convolution fusion | flops 1096810496 | bytes 13697024 | tf_op jit(solution)/shard_map/srab,acb->srcb/dot_general | solution.py:29
  213.9 4.5 %copy.48 = bf16[512,64,64]{0,2,1:T(8,128)(2,1)S(1)} copy(bf16[512,64,64]{0,1,2:T(8,128)(2,1)} %convert_reduce_fusion) | data formatting | bytes 8388608 | tf_op jit(solution)/shard_map/srw,wo->ro/reduce_sum | solution.py:42
  218.4 2.0 fusion.26
  220.5 90.1 %all-reduce.4.cloned.1.call-done = f32[512,128]{1,0:T(8,128)} async-done(((f32[512,128]{1,0:T(8,128)}), f32[512,128]{1,0:T(8,128)}) %all-reduce.4.cloned.1.call-update) | async-done | bytes 262160 | tf_op jit(solution)/shard_map/psum | solution.py:43
  310.5 1.3 dynamic-slice_multiply_fusion
  (36 shorter events, 0.7 us)
Async XLA Ops:
  6.5 211.9 %copy-start = (bf16[4096,128]{1,0:T(8,128)(2,1)S(1)}, bf16[4096,128]{1,0:T(8,128)(2,1)}, u32[]{:S(2)}) copy-start(bf16[4096,128]{1,0:T(8,128)(2,1)} %param.17) | copy-start | bytes 3145732
  6.5 178.4 %all-reduce.6.cloned.1.call-start = ((), (), s32[]{:S(2)}) async-start(), calls=%async_computation.1 | async-start | bytes 12582912 | tf_op jit(solution)/shard_map/psum | solution.py:11
  29.2 13.4 %copy-start.4 = (s32[6]{0:T(128)S(1)}, s32[6]{0:T(128)}, u32[]{:S(2)}) copy-start(s32[6]{0:T(128)} %param.11) | copy-start | bytes 76
  29.2 21.6 %copy-start.3 = (s32[2,6]{1,0:T(2,128)S(1)}, s32[2,6]{1,0:T(2,128)}, u32[]{:S(2)}) copy-start(s32[2,6]{1,0:T(2,128)} %param.13) | copy-start | bytes 148
  39.4 26.3 %copy-start.5 = (s32[512]{0:T(512)S(1)}, s32[512]{0:T(512)}, u32[]{:S(2)}) copy-start(s32[512]{0:T(512)} %param.10) | copy-start | bytes 6148
  42.3 268.2 %all-reduce.4.cloned.1.call-start = ((), (), s32[]{:S(2)}) async-start(), calls=%async_computation | async-start | bytes 524288 | tf_op jit(solution)/shard_map/psum | solution.py:43
  185.0 8.7 %copy-start.1 = (bf16[64,64,64]{0,1,2:T(8,128)(2,1)S(1)}, bf16[64,64,64]{0,1,2:T(8,128)(2,1)}, u32[]{:S(2)}) copy-start(bf16[64,64,64]{0,1,2:T(8,128)(2,1)} %get-tuple-element.14) | copy-start | bytes 1572868
  185.0 8.7 %copy-start.2 = (bf16[64,64,64]{0,1,2:T(8,128)(2,1)S(1)}, bf16[64,64,64]{0,1,2:T(8,128)(2,1)}, u32[]{:S(2)}) copy-start(bf16[64,64,64]{0,1,2:T(8,128)(2,1)} %get-tuple-element.15) | copy-start | bytes 1572868
Sparse Core Ops, SparseCore 0:
  42.4 142.4 all-reduce.5
  220.6 89.9 all-reduce.3
where the time goes:
time: 320 us; the launch traced here: 319 us
  waiting for transfers between devices  184 us (58%)
  local copies, waits for them, and re-layouts  67.4 us (21%)
  matrix products  30.9 us (10%)
  between operations  28.8 us (9%)
  other arithmetic  7.02 us (2%)
    psum x1, waiting for transfers between devices, spread(): return lax.psum(block, axis)  94.3 us
    psum x1, waiting for transfers between devices, local(): totals = lax.psum(partial_amps, 'slc')  90.1 us
    dot_general x3, matrix products, local(): jnp.einsum('srab,acb->srcb', states.reshape(slice_count, row_total, bond_...  28.9 us
    reshape x12, local copies, waits for them, and re-layouts, local(): branch.reshape(bond_dim, bond_dim, bond_dim)  28 us
    gather x2, local copies, waits for them, and re-layouts, local(): starts = jnp.take(boundary, bitstrings, axis=0)  17.9 us
  transfers between devices with their start and end apart: 2, of which 2 were waited for; matrix products, arithmetic and copies ran while one was open for 11% of the time, Pallas kernels for 0%

commit v1 on v0

v1 whole, which is shorter than its diff:
```python
import functools
import math

import jax
import jax.numpy as jnp
from jax import lax
from jax.experimental import pallas as pl
from jax.experimental.pallas import tpu as pltpu
from jax.sharding import PartitionSpec as P

F32 = jnp.float32
BF16 = jnp.bfloat16
TILE = 16


def iota(shape, dim):
    return lax.broadcasted_iota(jnp.int32, shape, dim)


def log2(value):
    assert value & (value - 1) == 0
    return value.bit_length() - 1


def one_hot(mask):
    return jnp.where(mask, 1.0, 0.0).astype(BF16)


def dot(x, y):
    return jnp.dot(x, y, preferred_element_type=F32)


def dot_t(x, y):
    return lax.dot_general(x, y, (((1,), (1,)), ((), ())), preferred_element_type=F32)


def split(x):
    high = x.astype(BF16)
    return high, (x - high.astype(F32)).astype(BF16)


def kernel(
    n, owners, tree, assign, bits, pool_hbm, tensors_hbm, boundary_hbm, closing_hbm, out,
    pool, tensors, boundary, closing, packed, got, pick, tables, starts, close,
    factors, states, partial, terms, load_sem, send_sem, recv_sem, send2_sem, recv2_sem,
):
    me = lax.axis_index("slc")
    bond, pair = pool.shape[1], pool.shape[2]
    share = bond // n
    width = bond * share
    half = width // 2
    sections, slices = tree.shape[0], assign.shape[0]
    notes = got.shape[1] - half
    rows = partial.shape[0]
    out_rows = rows // n
    span = bond * TILE // share
    chunks = pair // span

    loads = [
        pltpu.make_async_copy(source, target, load_sem.at[i])
        for i, (source, target) in enumerate(
            ((pool_hbm, pool), (tensors_hbm, tensors), (boundary_hbm, boundary), (closing_hbm, closing))
        )
    ]
    for load in loads:
        load.start()

    barrier = pltpu.get_barrier_semaphore()

    def greet(d, carry):
        pl.semaphore_signal(
            barrier, inc=1, device_id={"slc": lax.rem(me + d, n)}, device_id_type=pl.DeviceIdType.MESH
        )
        return carry

    lax.fori_loop(1, n, greet, 0)

    r, l = iota((span, span), 0), iota((span, span), 1)
    within = jnp.bitwise_and(r, TILE - 1)
    source = (
        jnp.right_shift(within, log2(share)) * bond
        + jnp.right_shift(r, log2(TILE)) * share
        + jnp.bitwise_and(r, share - 1)
    )
    order = one_hot(source == l)
    order = jnp.concatenate([order, order], axis=1)
    blank = jnp.zeros((bond, span), BF16)
    loads[0].wait()
    for i in range(chunks // 2):
        low = pool[0, :, i * span:(i + 1) * span]
        high = pool[0, :, pair // 2 + i * span:pair // 2 + (i + 1) * span]
        both = jnp.concatenate(
            [jnp.concatenate([low, blank], axis=0), jnp.concatenate([blank, high], axis=0)], axis=1
        )
        moved = dot_t(order, both).astype(BF16)
        for j in range(n):
            packed[j, i * TILE:(i + 1) * TILE, :] = moved[j * TILE:(j + 1) * TILE, :]
    note_row = iota((notes, 2 * bond), 0)
    note = jnp.zeros((notes, 2 * bond), F32)
    for k in range(sections):
        for s in range(slices):
            note = jnp.where(note_row == k * slices + s, assign[s, k].astype(F32), note)
    note = note.astype(BF16)
    for j in range(n):
        packed[j, half:, :] = note
    got[me] = packed[me]

    pl.semaphore_wait(barrier, n - 1)

    def exchange(d):
        peer = lax.rem(me + d, n)
        return pltpu.make_async_remote_copy(
            src_ref=packed.at[peer],
            dst_ref=got.at[me],
            send_sem=send_sem.at[d],
            recv_sem=recv_sem.at[d],
            device_id={"slc": peer},
            device_id_type=pl.DeviceIdType.MESH,
        )

    def start(d, carry):
        exchange(d).start()
        return carry

    lax.fori_loop(1, n, start, 0)

    lane = iota((span, width), 1)
    wanted = (
        jnp.right_shift(lane, log2(share)) * bond + me * share + jnp.bitwise_and(lane, share - 1)
    )
    for i in range(chunks):
        pick[i * span:(i + 1) * span, :] = one_hot(iota((span, width), 0) + i * span == wanted)
    loads[1].wait()
    for k in range(sections):
        tables[k] = dot(tensors[k], pick[...]).astype(BF16)
    bits_row = bits[...].astype(F32)
    eye = iota((rows, rows), 0) == iota((rows, rows), 1)
    bits_col = jnp.sum(jnp.where(eye, bits_row, 0.0), axis=1, keepdims=True)
    states_of = one_hot(bits_col == iota((rows, boundary.shape[0]), 1).astype(F32))
    loads[2].wait()
    taken = dot(boundary[...], pick[...]).astype(BF16)
    starts[...] = dot(states_of, taken).astype(BF16)
    r, l = iota((TILE, span), 0), iota((TILE, span), 1)
    keep = one_hot(
        l == jnp.right_shift(r, log2(share)) * bond + me * share + jnp.bitwise_and(r, share - 1)
    )
    loads[3].wait()
    for i in range(chunks):
        close[i * TILE:(i + 1) * TILE, :] = dot(keep, closing[i * span:(i + 1) * span, :]).astype(BF16)

    lane_b = jnp.bitwise_and(iota((width, width), 1), share - 1)
    same_b = jnp.bitwise_and(iota((width, width), 0), share - 1) == lane_b
    r, l = iota((2 * bond, width), 0), jnp.right_shift(iota((2 * bond, width), 1), log2(share))
    widen_low, widen_high = one_hot(r == l), one_hot(r == l + bond)
    r, l = iota((bond, 2 * bond), 0), iota((bond, 2 * bond), 1)
    turn_low, turn_high = one_hot(r == l), one_hot(r + bond == l)

    def finish(d, carry):
        exchange(d).wait()
        return carry

    lax.fori_loop(1, n, finish, 0)

    values = got[:, half:, :].reshape(n * notes, 2 * bond).astype(F32)
    chosen = one_hot(values == iota((n * notes, 2 * bond), 1).astype(F32))[:, :bond]
    for k in range(sections):
        factors[k] = dot(chosen, tables[tree[k]])

    group = min(n, 8)
    block = got[owners[0]][:half]
    first = jnp.concatenate([dot_t(turn_low, block), dot_t(turn_high, block)], axis=1)

    def factor_of(k, g, i, s):
        line = factors[k, pl.ds(pl.multiple_of((g * group + i) * notes, notes), notes), :]
        return line[k * slices + s:k * slices + s + 1, :]

    step_rows = group * slices * bond
    for g in range(n // group):
        for i in range(group):
            for s in range(slices):
                at = g * step_rows + (i * slices + s) * bond
                states[at:at + bond, :] = (first * factor_of(0, g, i, s)).astype(BF16)

    total = jnp.zeros((bond, width), F32)
    for k in range(1, sections):
        block = got[owners[k]][:half]
        spread = jnp.concatenate([dot(block, widen_low), dot(block, widen_high)], axis=0)
        branch = jnp.where(same_b, spread, 0.0).astype(BF16)

        def advance(g, sofar, k=k, branch=branch):
            base = pl.multiple_of(g * step_rows, step_rows)
            product = dot_t(states[pl.ds(base, step_rows), :], branch)
            for i in range(group):
                for s in range(slices):
                    at = (i * slices + s) * bond
                    scaled = product[at:at + bond, :] * factor_of(k, g, i, s)
                    if k < sections - 1:
                        states[pl.ds(pl.multiple_of(base + at, bond), bond), :] = scaled.astype(BF16)
                    else:
                        sofar = sofar + scaled
            return sofar

        total = lax.fori_loop(0, n // group, advance, total)

    r, l = iota((width, bond), 0), iota((width, bond), 1)
    repeat = one_hot(jnp.right_shift(r, log2(share)) == l)
    weights = jnp.zeros((width, close.shape[1]), F32)
    for piece in split(total):
        wide = jnp.where(same_b, dot(repeat, piece), 0.0).astype(BF16)
        weights = weights + dot(wide, close[...])
    high, low = split(weights)
    partial[...] = dot(starts[...], high) + dot(starts[...], low)
    terms[me] = partial[pl.ds(pl.multiple_of(me * out_rows, out_rows), out_rows), :]

    def gather(d):
        peer = lax.rem(me + d, n)
        return pltpu.make_async_remote_copy(
            src_ref=partial.at[pl.ds(pl.multiple_of(peer * out_rows, out_rows), out_rows), :],
            dst_ref=terms.at[me],
            send_sem=send2_sem.at[d],
            recv_sem=recv2_sem.at[d],
            device_id={"slc": peer},
            device_id_type=pl.DeviceIdType.MESH,
        )

    def start2(d, carry):
        gather(d).start()
        return carry

    lax.fori_loop(1, n, start2, 0)

    def finish2(d, carry):
        gather(d).wait()
        return carry

    lax.fori_loop(1, n, finish2, 0)
    out[...] = jnp.sum(terms[...], axis=0) * (1.0 / math.sqrt(slices * n))


def local(
    n, bitstrings, tree_order, owners, slice_assign, boundary, branch_pool, slice_tensors, closing
):
    slices, sections = slice_assign.shape
    bond, pair = branch_pool.shape[1:]
    rows, outs = bitstrings.shape[0], closing.shape[1]
    share = bond // n
    width = bond * share
    notes = -(-slices * sections // TILE) * TILE
    smem = pl.BlockSpec(memory_space=pltpu.SMEM)
    vmem = pl.BlockSpec(memory_space=pltpu.VMEM)
    anywhere = pl.BlockSpec(memory_space=pl.ANY)
    return pl.pallas_call(
        functools.partial(kernel, n),
        out_shape=jax.ShapeDtypeStruct((rows // n, outs), F32),
        in_specs=[smem, smem, smem, vmem, anywhere, anywhere, anywhere, anywhere],
        out_specs=vmem,
        scratch_shapes=[
            pltpu.VMEM(branch_pool.shape, BF16),
            pltpu.VMEM(slice_tensors.shape, BF16),
            pltpu.VMEM(boundary.shape, BF16),
            pltpu.VMEM(closing.shape, BF16),
            pltpu.VMEM((n, width // 2 + notes, 2 * bond), BF16),
            pltpu.VMEM((n, width // 2 + notes, 2 * bond), BF16),
            pltpu.VMEM((pair, width), BF16),
            pltpu.VMEM((sections, bond, width), BF16),
            pltpu.VMEM((rows, width), BF16),
            pltpu.VMEM((width, outs), BF16),
            pltpu.VMEM((sections, n * notes, width), F32),
            pltpu.VMEM((n * slices * bond, width), BF16),
            pltpu.VMEM((rows, outs), F32),
            pltpu.VMEM((n, rows // n, outs), F32),
            pltpu.SemaphoreType.DMA((4,)),
            pltpu.SemaphoreType.DMA((n,)),
            pltpu.SemaphoreType.DMA((n,)),
            pltpu.SemaphoreType.DMA((n,)),
            pltpu.SemaphoreType.DMA((n,)),
        ],
        compiler_params=pltpu.CompilerParams(collective_id=0, has_side_effects=True),
    )(
        owners, tree_order, slice_assign, bitstrings.reshape(1, rows),
        branch_pool, slice_tensors, boundary, closing,
    )


def solution(mesh):
    return jax.shard_map(
        functools.partial(local, mesh.shape["slc"]),
        mesh=mesh,
        in_specs=(
            P("grp"),
            P("grp"),
            P("grp"),
            P(("grp", "slc"), None),
            P("grp", None),
            P(("grp", "slc"), None, None),
            P("grp", None, None),
            P("grp", None),
        ),
        out_specs=P(("grp", "slc"), None),
        check_vma=False,
    )
```

time: 320 us -> 34.2 us (0.11)
  waiting for transfers between devices: 184 us -> 0 us
  local copies, waits for them, and re-layouts: 67.4 us -> 1.32 us
  Pallas kernels: 0 us -> 32.6 us
  matrix products: 30.9 us -> 0 us
  between operations: 28.8 us -> 0.01 us
  other arithmetic: 7.02 us -> 0 us
    psum x2 -> x0, waiting for transfers between devices: 184 us -> none  [the longest x1 94.3 us: spread(): return lax.psum(block, axis)]
    pallas_call x0 -> x1, Pallas kernels: none -> 32.6 us  [local(): pl.pallas_call(functools.partial(kernel, n), out_shape=jax.ShapeDtypeStru...]
    dot_general x4 -> x0, matrix products: 30.9 us -> none  [the longest x3 28.9 us: local(): jnp.einsum('srab,acb->srcb', states.reshape(slice_count, row_total, bond_...]
    reshape x12 -> x0, local copies, waits for them, and re-layouts: 28 us -> none  [local(): branch.reshape(bond_dim, bond_dim, bond_dim)]
    gather x8 -> x0, local copies, waits for them, and re-layouts: 23.7 us -> none  [the longest x2 17.9 us: local(): starts = jnp.take(boundary, bitstrings, axis=0)]
    select_n x6 -> x0, other arithmetic: 5.12 us -> none  [the longest x2 2.7 us: local(): starts = jnp.take(boundary, bitstrings, axis=0)]
    reduce_sum x1 -> x0, local copies, waits for them, and re-layouts: 4.53 us -> none  [local(): jnp.einsum('srw,wo->ro', states, closing, preferred_element_type=jnp.floa...]
    select_n x1 -> x0, local copies, waits for them, and re-layouts: 4.37 us -> none  [local(): starts = jnp.take(boundary, bitstrings, axis=0)]
  transfers between devices with their start and end apart: 2 -> 0, of which waited for: 2 -> 0; matrix products, arithmetic and copies ran while one was open for 11% -> 0% of each run, Pallas kernels for 0% -> 0%
where the time goes in v1:
time: 34.2 us; the launch traced here: 34 us
  Pallas kernels  32.6 us (95%)
  local copies, waits for them, and re-layouts  1.32 us (4%)
    pallas_call x1, Pallas kernels, local(): pl.pallas_call(functools.partial(kernel, n), out_shape=jax.ShapeDtypeStru...  32.6 us
    unnamed x1, local copies, waits for them, and re-layouts  1.32 us

profile of v1, /device:TPU:0, one launch (start us, length us, event | category | flops | bytes accessed | tf_op | source)
XLA Modules:
  0.0 34.0 jit_solution(2828217297101494096)
XLA Ops:
  0.0 32.6 %shard_map.82 = f32[32,128]{1,0:T(8,128)} custom-call(s32[6]{0:T(128)} %owners.1, s32[6]{0:T(128)} %tree.1, s32[2,6]{1,0:T(2,128)} %assign.1, s32[1,512]{1,0:T(1,128)} %bitcast.1, bf16[1,64,4096]{2,1,0:T(8,128)(2,1)} %pool_hbm.1, bf16[6,64,4096]{2,1,0:T(8,128)(2,1)} %tensors_hbm.1, bf16[512,4096]{1,0:T(8,128)(2,1)} %boundary_hbm.1, bf16[4096,128]{1,0:T(8,128)(2,1)} %closing_hbm.1), custom_call_target="tpu_custom_call" | custom-call | tf_op jit(solution)/shard_map/pallas_call | solution.py:252
  32.6 1.3 %copy.10 = f32[32,128]{1,0:T(8,128)} copy(f32[32,128]{1,0:T(8,128)} %shard_map.82) | data formatting | bytes 32768
